TPU v7x, 256 devices: a whole 4x4x8 slice. The times are simulated.
256 devices in a mesh: prow: 32 (over x, z), pcol: 8 (over y, core).
Axes of the slice: x: 4, y: 4, z: 8, core: 2. Of those that a mesh axis runs over, the one named last changes fastest.
Arguments:
- anc_inverse: bfloat16 [4, 32, 256, 16, 8, 256], P(None, 'prow', None, None, 'pcol'), may hold values from -6 to 6
- first_lower: bfloat16 [4, 32, 256, 256], P(None, 'prow', 'pcol'), may hold values from -0.046875 to 0.046875
- second_lower: bfloat16 [4, 32, 256, 256], P(None, 'prow', 'pcol'), may hold values from -0.0546875 to 0.0546875
- second_top: bfloat16 [256, 256], replicated, may hold values from -0.3125 to 0.3125
- struct_first: int32 [128], replicated, may hold values from 0 to 1
- struct_keep: int32 [128], replicated, may hold values from 0 to 1
- pivot_h: float32 [2, 256, 256], replicated, as said below
- pivot_s: float32 [2, 256, 256], replicated, as said below
- shifts: float32 [40], replicated, may hold values from 0.5 to 4
- pole_index: int32 [40], replicated, may hold values from 0 to 39, each once
Outputs:
- first_column: bfloat16 [4, 32, 256, 256], P(None, 'prow', 'pcol')
- first_diag: float32 [256, 256], replicated
- link_column: bfloat16 [256, 256], replicated
- second_column: bfloat16 [4, 32, 256, 256], P(None, 'prow', 'pcol')
- second_diag: float32 [256, 256], replicated
Inputs may be any that keep to these rules, and one draw needn't show every extreme that they name: `struct_first`: 1 marks a block row of the first supernode's structure. `struct_keep`: 1 marks a structure block that the second supernode keeps. `pole_index`: each pole appears once. `pivot_h`: symmetric, with a positive diagonal larger than each row's off-diagonal magnitudes together. `pivot_s`: symmetric, with a positive diagonal larger than each row's off-diagonal magnitudes together.
All inputs are finite; a program needn't handle non-finite values.
Results may differ from a plain program's by a relative error of at most 0.0041.
The roundings to bfloat16 on the way count: a program that leaves them out, or rounds other values in their place, can miss the bound.
Values may be sent and summed in bfloat16 or wider, within the bound.
A program may use at most 64 MiB of HBM per device.

v0:
```python
import jax
import jax.numpy as jnp
from jax import lax
from jax.sharding import PartitionSpec as P


def pivot_inverse(h_block, s_block, shift):
    factor = jnp.linalg.cholesky(h_block + shift * s_block)
    identity = jnp.eye(h_block.shape[0], dtype=jnp.float32)
    return jax.scipy.linalg.cho_solve((factor, True), identity)


def local_mask(flags, row_blocks, grid_rows, my_row):
    table = flags.reshape(row_blocks, grid_rows).astype(jnp.float32)
    return lax.dynamic_index_in_dim(table, my_row, axis=1, keepdims=False)


def per_device(
    anc_inverse,
    first_lower,
    second_lower,
    second_top,
    struct_first,
    struct_keep,
    pivot_h,
    pivot_s,
    shifts,
    pole_index,
):
    grid_rows = lax.axis_size("prow")
    grid_cols = lax.axis_size("pcol")
    my_row = lax.axis_index("prow")
    my_col = lax.axis_index("pcol")
    row_blocks = first_lower.shape[0]
    slab = first_lower.shape[2]
    width = first_lower.shape[3]
    col_blocks = anc_inverse.shape[3]
    first_mask = local_mask(struct_first, row_blocks, grid_rows, my_row)
    second_mask = first_mask * local_mask(struct_keep, row_blocks, grid_rows, my_row)
    lower_first = first_lower[:, 0] * first_mask.astype(jnp.bfloat16)[:, None, None]
    lower_second = second_lower[:, 0] * second_mask.astype(jnp.bfloat16)[:, None, None]
    stacked = jnp.concatenate([lower_first, lower_second], axis=2)[:, None]
    gathered = lax.all_gather(stacked, "prow", axis=1, tiled=True)
    grouped = gathered.reshape(row_blocks, grid_rows // grid_cols, grid_cols, slab, 2 * width)
    columns = lax.all_to_all(grouped, "pcol", split_axis=2, concat_axis=3, tiled=True)
    column_blocks = columns.reshape(col_blocks, width, 2 * width)
    inverse_rows = anc_inverse.reshape(row_blocks, width, col_blocks, width)
    totals = lax.psum(
        jnp.einsum(
            "axcy,cyz->xaz", inverse_rows, column_blocks, preferred_element_type=jnp.float32
        ),
        "pcol",
    )
    row_part = lax.dynamic_slice_in_dim(totals, my_col * slab, slab, 0)
    first_col = (-row_part[:, :, :width] * first_mask[None, :, None]).astype(jnp.bfloat16)
    bridge = jnp.einsum("raw,wz->raz", first_col, second_top, preferred_element_type=jnp.float32)
    second_col = (-(row_part[:, :, width:] + bridge) * second_mask[None, :, None]).astype(
        jnp.bfloat16
    )
    first_rows = lower_first.transpose(1, 0, 2)
    second_rows = lower_second.transpose(1, 0, 2)
    first_term = jnp.einsum(
        "ray,raz->yz", first_rows, first_col, preferred_element_type=jnp.float32
    )
    cross_term = jnp.einsum(
        "ray,raz->yz", first_col, second_rows, preferred_element_type=jnp.float32
    )
    second_term = jnp.einsum(
        "ray,raz->yz", second_rows, second_col, preferred_element_type=jnp.float32
    )
    first_sum, cross_sum, second_sum = lax.psum(
        (first_term, cross_term, second_term), ("prow", "pcol")
    )
    poles = jnp.arange(shifts.shape[0], dtype=jnp.int32)
    shift = jnp.sum(jnp.where(poles == pole_index[0], shifts, 0.0))
    first_diag = pivot_inverse(pivot_h[0], pivot_s[0], shift) - first_sum
    link_col = (
        -(
            cross_sum
            + jnp.dot(
                first_diag.astype(jnp.bfloat16), second_top, preferred_element_type=jnp.float32
            )
        )
    ).astype(jnp.bfloat16)
    second_diag = (
        pivot_inverse(pivot_h[1], pivot_s[1], shift)
        - second_sum
        - jnp.einsum("yz,yw->zw", second_top, link_col, preferred_element_type=jnp.float32)
    )
    return (
        first_col.transpose(1, 0, 2)[:, None],
        first_diag,
        link_col,
        second_col.transpose(1, 0, 2)[:, None],
        second_diag,
    )


def solution(mesh):
    return jax.shard_map(
        per_device,
        mesh=mesh,
        in_specs=(
            P(None, "prow", None, None, "pcol", None),
            P(None, "prow", "pcol", None),
            P(None, "prow", "pcol", None),
            P(),
            P(),
            P(),
            P(),
            P(),
            P(),
            P(),
        ),
        out_specs=(P(None, "prow", "pcol", None), P(), P(), P(None, "prow", "pcol", None), P()),
        check_vma=False,
    )
```

profile of v0, /device:TPU:8, one launch (start us, length us, event | category | flops | bytes accessed | tf_op | source)
XLA Modules:
  0.0 544.1 jit_solution(14048645056738182097)
XLA Ops:
  7.2 0.7 convert_element_type.47
  8.0 0.7 convert_element_type.44
  9.0 0.9 bitcast_multiply_fusion
  9.9 0.9 bitcast_multiply_fusion.1
  10.8 0.7 pad_maximum_fusion
  11.5 1.1 fusion.48
  12.7 1.1 fusion.47
  13.9 1.9 fusion.43
  15.8 0.7 fusion.23
  16.9 0.7 fusion.22
  17.7 0.7 fusion.11
  18.5 11.7 %cholesky.130 = f32[128,128]{1,0:T(8,128)S(1)} custom-call(f32[128,128]{1,0:T(8,128)S(1)} %cholesky.194), custom_call_target="Cholesky" | custom-call | tf_op jit(solution)/shard_map/jit(cholesky)/cholesky | solution.py:8
  30.3 9.8 %custom-call.15 = f32[1,128,128]{1,2,0:T(8,128)S(1)} custom-call(f32[1,128,128]{2,1,0:T(8,128)S(1)} %get-tuple-element.84), custom_call_target="InvertDiagBlocksLowerTriangular" | custom-call | tf_op jit(solution)/shard_map/jit(cholesky)/cholesky | solution.py:8
  40.6 11.7 %cholesky.147 = f32[128,128]{1,0:T(8,128)S(1)} custom-call(f32[128,128]{1,0:T(8,128)S(1)} %convolution_subtract_fusion.5), custom_call_target="Cholesky" | custom-call | tf_op jit(solution)/shard_map/jit(cholesky)/cholesky | solution.py:8
  52.3 0.6 compare_reduce_fusion.3
  53.0 0.6 compare_reduce_fusion.2
  55.0 41.5 %all-gather.3.cloned.1.call-done = bf16[4,1024,512]{2,1,0:T(8,128)(2,1)} async-done(((bf16[4,32,512]{2,1,0:T(8,128)(2,1)}), bf16[4,1024,512]{2,1,0:T(8,128)(2,1)}) %all-gather.3.cloned.1.call-update) | async-done | bytes 4194320 | tf_op jit(solution)/shard_map/all_gather | solution.py:43
  96.5 4.7 copy.82
  101.2 5.2 all-to-all-start
  106.4 4.0 while.4
  106.5 0.6 fusion.74
  107.0 1.4 bitcast_dynamic-update-slice_fusion.4
  108.5 0.6 fusion.74
  109.0 1.4 bitcast_dynamic-update-slice_fusion.4
  110.4 19.7 %custom-call.16 = f32[2,128,128]{1,2,0:T(8,128)S(1)} custom-call(f32[2,128,128]{2,1,0:T(8,128)S(1)} %get-tuple-element.21), custom_call_target="InvertDiagBlocksLowerTriangular" | custom-call | tf_op jit(solution)/shard_map/jit(_cho_solve)/triangular_solve | solution.py:10
  130.1 11.7 %cholesky.164 = f32[128,128]{1,0:T(8,128)S(1)} custom-call(f32[128,128]{1,0:T(8,128)S(1)} %cholesky.197), custom_call_target="Cholesky" | custom-call | tf_op jit(solution)/shard_map/jit(cholesky)/cholesky | solution.py:8
  141.9 9.8 %custom-call.17 = f32[1,128,128]{1,2,0:T(8,128)S(1)} custom-call(f32[1,128,128]{2,1,0:T(8,128)S(1)} %get-tuple-element.80), custom_call_target="InvertDiagBlocksLowerTriangular" | custom-call | tf_op jit(solution)/shard_map/jit(cholesky)/cholesky | solution.py:8
  152.2 11.7 %cholesky.181 = f32[128,128]{1,0:T(8,128)S(1)} custom-call(f32[128,128]{1,0:T(8,128)S(1)} %convolution_subtract_fusion.4), custom_call_target="Cholesky" | custom-call | tf_op jit(solution)/shard_map/jit(cholesky)/cholesky | solution.py:8
  163.9 0.6 compare_reduce_fusion.1
  164.6 0.6 compare_reduce_fusion
  166.6 4.0 while.5
  167.2 1.4 bitcast_dynamic-update-slice_fusion.5
  168.6 0.6 fusion.75
  169.2 1.4 bitcast_dynamic-update-slice_fusion.5
  170.6 19.9 %custom-call.18 = f32[2,128,128]{1,2,0:T(8,128)S(1)} custom-call(f32[2,128,128]{2,1,0:T(8,128)S(1)} %get-tuple-element.22), custom_call_target="InvertDiagBlocksLowerTriangular" | custom-call | tf_op jit(solution)/shard_map/jit(_cho_solve)/triangular_solve | solution.py:10
  192.3 2.5 copy.83
  194.8 9.6 %fusion.2 = f32[256,4,512]{2,0,1:T(8,128)} fusion(bf16[16,256,512,1]{2,1,0,3:T(8,128)(2,1)S(1)} %bitcast.134, bf16[4,256,16,256]{3,2,1,0:T(8,128)(2,1)} %bitcast.136), kind=kOutput, calls=%fused_computation.6 | convolution fusion | flops 4294967296 | bytes 14680064 | tf_op jit(solution)/shard_map/axcy,cyz->xaz/dot_general | solution.py:49
  206.0 64.4 %all-reduce.5.cloned.1.call-done = f32[256,4,512]{2,0,1:T(8,128)} async-done(((f32[256,4,512]{2,0,1:T(8,128)}), f32[256,4,512]{2,0,1:T(8,128)}) %all-reduce.5.cloned.1.call-update) | async-done | bytes 2097168 | tf_op jit(solution)/shard_map/psum | solution.py:48
  270.3 1.0 fusion.15
  271.3 0.9 convolution_bitcast_fusion.3
  272.2 0.9 convolution_bitcast_fusion.2
  273.1 1.1 fusion.10
  274.2 0.9 convolution_bitcast_fusion.1
  275.5 1.6 fusion.71
  277.1 256.3 %all-reduce.7.cloned.1.call-done = (f32[256,256]{1,0:T(8,128)}, f32[256,256]{1,0:T(8,128)}, f32[256,256]{1,0:T(8,128)}) async-done(((f32[256,256]{1,0:T(8,128)}, f32[256,256]{1,0:T(8,128)}, f32[256,256]{1,0:T(8,128)}), (f32[256,256]{1,0:T(8,128)}, f32[256,256]{1,0:T(8,128)}, f32[256,256]{1,0:T(8,128)})) %all-reduce.7.cloned.1.call-update) | async-done | bytes 786448 | tf_op jit(solution)/shard_map/psum | solution.py:71
  533.4 1.0 maximum_subtract_fusion
  534.4 1.2 fusion.7
  535.6 1.9 fusion.6
  (61 shorter events, 6.7 us)
Async XLA Ops:
  7.2 266.0 %copy-start = (bf16[256,256]{1,0:T(8,128)(2,1)S(1)}, bf16[256,256]{1,0:T(8,128)(2,1)}, u32[]{:S(2)}) copy-start(bf16[256,256]{1,0:T(8,128)(2,1)} %param.16) | copy-start | bytes 393220
  7.2 89.3 %all-gather.3.cloned.1.call-start = ((), (), s32[]{:S(2)}) async-start(), calls=%async_computation.2 | async-start | bytes 4325376 | tf_op jit(solution)/shard_map/all_gather | solution.py:43
  101.2 91.1 %all-to-all-start = ((bf16[4,4,8,32,512]{4,3,1,0,2:T(8,128)(2,1)}), bf16[4,4,8,32,512]{4,3,1,0,2:T(8,128)(2,1)}, u32[]{:S(2)}, u32[]{:S(2)}) async-start(bf16[4,4,8,32,512]{4,3,1,0,2:T(8,128)(2,1)} %copy.82), calls=%async_computation | async-start | bytes 8388608 | tf_op jit(solution)/shard_map/all_to_all | solution.py:45
  106.4 164.0 %all-reduce.5.cloned.1.call-start = ((), (), s32[]{:S(2)}) async-start(), calls=%async_computation.1 | async-start | bytes 4194304 | tf_op jit(solution)/shard_map/psum | solution.py:48
  204.4 329.0 %all-reduce.7.cloned.1.call-start = ((), (), s32[]{:S(2)}) async-start(), calls=%async_computation.3 | async-start | bytes 1572864 | tf_op jit(solution)/shard_map/psum | solution.py:71
  274.2 263.3 %copy-start.3 = (bf16[32,4,256]{2,0,1:T(8,128)(2,1)}, bf16[32,4,256]{2,0,1:T(8,128)(2,1)S(1)}, u32[]{:S(2)}) copy-start(bf16[32,4,256]{2,0,1:T(8,128)(2,1)S(1)} %fusion.10) | copy-start | bytes 196612
  534.4 3.2 copy-start.1
  535.6 2.0 copy-start.2
Sparse Core Ops, SparseCore 0:
  11.6 84.8 all-gather.2
  204.5 65.7 all-reduce.4
  276.7 256.6 all-reduce.6
where the time goes:
time: 545 us; the launch traced here: 544 us
  waiting for transfers between devices  362 us (66%)
  other arithmetic  120 us (22%)
  matrix products  20.9 us (4%)
  local copies, waits for them, and re-layouts  18.6 us (3%)
  between operations  16.7 us (3%)
    psum x1, waiting for transfers between devices, per_device(): lax.psum((first_term, cross_term, second_term), ('prow', 'pcol'))  256 us
    another operation x14, other arithmetic, pivot_inverse(): factor = jnp.linalg.cholesky(h_block + shift * s_block)  69.2 us
    psum x1, waiting for transfers between devices, per_device(): lax.psum(jnp.einsum('axcy,cyz->xaz', inverse_rows, column_blocks, preferr...  64.4 us
    all_gather x1, waiting for transfers between devices, per_device(): gathered = lax.all_gather(stacked, 'prow', axis=1, tiled=True)  41.5 us
    another operation x5, other arithmetic, pivot_inverse(): return jax.scipy.linalg.cho_solve((factor, True), identity)  39.6 us
  transfers between devices with their start and end apart: 4, of which 3 were waited for; matrix products, arithmetic and copies ran while one was open for 24% of the time, Pallas kernels for 0%

commit v1 on v0

--- a/solution.py
+++ b/solution.py
@@ -2,6 +2,12 @@
 import jax.numpy as jnp
 from jax import lax
 from jax.sharding import PartitionSpec as P
+
+
+def apply_wires(arr):
+    for d in ("pcol", "prow"):
+        arr = lax.psum(arr, d)
+    return arr
 
 
 def pivot_inverse(h_block, s_block, shift):
@@ -68,9 +74,7 @@
     second_term = jnp.einsum(
         "ray,raz->yz", second_rows, second_col, preferred_element_type=jnp.float32
     )
-    first_sum, cross_sum, second_sum = lax.psum(
-        (first_term, cross_term, second_term), ("prow", "pcol")
-    )
+    first_sum, cross_sum, second_sum = apply_wires((first_term, cross_term, second_term))
     poles = jnp.arange(shifts.shape[0], dtype=jnp.int32)
     shift = jnp.sum(jnp.where(poles == pole_index[0], shifts, 0.0))
     first_diag = pivot_inverse(pivot_h[0], pivot_s[0], shift) - first_sum

time: 545 us -> 489 us (0.90)
  waiting for transfers between devices: 362 us -> 307 us
    psum x1 -> x2, waiting for transfers between devices: 256 us -> 218 us  [apply_wires(): arr = lax.psum(arr, d)]
    psum x1, waiting for transfers between devices: 64.4 us -> 44.7 us  [per_device(): lax.psum(jnp.einsum('axcy,cyz->xaz', inverse_rows, column_blocks, preferr...]
  transfers between devices with their start and end apart: 4 -> 5, of which waited for: 3 -> 4; matrix products, arithmetic and copies ran while one was open for 24% -> 27% of each run, Pallas kernels for 0% -> 0%
where the time goes in v1:
time: 489 us; the launch traced here: 488 us
  waiting for transfers between devices  307 us (63%)
  other arithmetic  120 us (25%)
  matrix products  21.2 us (4%)
  local copies, waits for them, and re-layouts  18.6 us (4%)
  between operations  16.8 us (3%)
  starting transfers between devices  5.09 us (1%)
    psum x2, waiting for transfers between devices, apply_wires(): arr = lax.psum(arr, d)  218 us
    another operation x14, other arithmetic, pivot_inverse(): factor = jnp.linalg.cholesky(h_block + shift * s_block)  69.2 us
    psum x1, waiting for transfers between devices, per_device(): lax.psum(jnp.einsum('axcy,cyz->xaz', inverse_rows, column_blocks, preferr...  44.7 us
    all_gather x1, waiting for transfers between devices, per_device(): gathered = lax.all_gather(stacked, 'prow', axis=1, tiled=True)  43.5 us
    another operation x5, other arithmetic, pivot_inverse(): return jax.scipy.linalg.cho_solve((factor, True), identity)  39.4 us
    dot_general x1, matrix products, per_device(): jnp.einsum('axcy,cyz->xaz', inverse_rows, column_blocks, preferred_elemen...  9.81 us
  transfers between devices with their start and end apart: 5, of which 4 were waited for; matrix products, arithmetic and copies ran while one was open for 27% of the time, Pallas kernels for 0%

profile of v1, /device:TPU:8, one launch (start us, length us, event | category | flops | bytes accessed | tf_op | source)
XLA Modules:
  0.0 488.3 jit_solution(17860784170273717539)
XLA Ops:
  7.2 0.7 convert_element_type.47
  8.0 0.7 convert_element_type.44
  9.0 0.9 bitcast_multiply_fusion
  9.9 0.9 bitcast_multiply_fusion.1
  10.8 0.7 pad_maximum_fusion
  11.5 1.1 fusion.48
  12.7 1.1 fusion.47
  13.9 1.9 fusion.43
  15.8 0.7 fusion.23
  16.9 0.7 fusion.22
  17.7 0.7 fusion.11
  18.5 11.7 %cholesky.130 = f32[128,128]{1,0:T(8,128)S(1)} custom-call(f32[128,128]{1,0:T(8,128)S(1)} %cholesky.194), custom_call_target="Cholesky" | custom-call | tf_op jit(solution)/shard_map/jit(cholesky)/cholesky | solution.py:14
  30.3 9.8 %custom-call.15 = f32[1,128,128]{1,2,0:T(8,128)S(1)} custom-call(f32[1,128,128]{2,1,0:T(8,128)S(1)} %get-tuple-element.87), custom_call_target="InvertDiagBlocksLowerTriangular" | custom-call | tf_op jit(solution)/shard_map/jit(cholesky)/cholesky | solution.py:14
  40.6 11.7 %cholesky.147 = f32[128,128]{1,0:T(8,128)S(1)} custom-call(f32[128,128]{1,0:T(8,128)S(1)} %convolution_subtract_fusion.5), custom_call_target="Cholesky" | custom-call | tf_op jit(solution)/shard_map/jit(cholesky)/cholesky | solution.py:14
  52.3 0.6 compare_reduce_fusion.3
  53.0 43.5 %all-gather.3.cloned.1.call-done = bf16[4,1024,512]{2,1,0:T(8,128)(2,1)} async-done(((bf16[4,32,512]{2,1,0:T(8,128)(2,1)}), bf16[4,1024,512]{2,1,0:T(8,128)(2,1)}) %all-gather.3.cloned.1.call-update) | async-done | bytes 4194320 | tf_op jit(solution)/shard_map/all_gather | solution.py:49
  96.5 4.7 copy.82
  101.2 5.0 %all-to-all-start = ((bf16[4,4,8,32,512]{4,3,1,0,2:T(8,128)(2,1)}), bf16[4,4,8,32,512]{4,3,1,0,2:T(8,128)(2,1)}, u32[]{:S(2)}, u32[]{:S(2)}) async-start(bf16[4,4,8,32,512]{4,3,1,0,2:T(8,128)(2,1)} %copy.82), calls=%async_computation | async-start | bytes 8388608 | tf_op jit(solution)/shard_map/all_to_all | solution.py:51
  106.2 0.6 compare_reduce_fusion.2
  108.2 4.0 while.4
  108.3 0.6 fusion.74
  108.8 1.4 bitcast_dynamic-update-slice_fusion.4
  110.9 1.4 bitcast_dynamic-update-slice_fusion.4
  112.2 19.7 %custom-call.16 = f32[2,128,128]{1,2,0:T(8,128)S(1)} custom-call(f32[2,128,128]{2,1,0:T(8,128)S(1)} %get-tuple-element.21), custom_call_target="InvertDiagBlocksLowerTriangular" | custom-call | tf_op jit(solution)/shard_map/jit(_cho_solve)/triangular_solve | solution.py:16
  131.9 11.7 %cholesky.164 = f32[128,128]{1,0:T(8,128)S(1)} custom-call(f32[128,128]{1,0:T(8,128)S(1)} %cholesky.197), custom_call_target="Cholesky" | custom-call | tf_op jit(solution)/shard_map/jit(cholesky)/cholesky | solution.py:14
  143.7 9.8 %custom-call.17 = f32[1,128,128]{1,2,0:T(8,128)S(1)} custom-call(f32[1,128,128]{2,1,0:T(8,128)S(1)} %get-tuple-element.83), custom_call_target="InvertDiagBlocksLowerTriangular" | custom-call | tf_op jit(solution)/shard_map/jit(cholesky)/cholesky | solution.py:14
  154.0 11.7 %cholesky.181 = f32[128,128]{1,0:T(8,128)S(1)} custom-call(f32[128,128]{1,0:T(8,128)S(1)} %convolution_subtract_fusion.4), custom_call_target="Cholesky" | custom-call | tf_op jit(solution)/shard_map/jit(cholesky)/cholesky | solution.py:14
  165.7 0.6 compare_reduce_fusion.1
  166.4 0.6 compare_reduce_fusion
  169.0 4.0 while.5
  169.6 1.4 bitcast_dynamic-update-slice_fusion.5
  171.0 0.6 fusion.75
  171.6 1.4 bitcast_dynamic-update-slice_fusion.5
  173.0 2.5 copy.83
  175.5 9.8 %fusion.2 = f32[256,4,512]{2,0,1:T(8,128)} fusion(bf16[16,256,512,1]{2,1,0,3:T(8,128)(2,1)S(1)} %bitcast.134, bf16[4,256,16,256]{3,2,1,0:T(8,128)(2,1)} %bitcast.136), kind=kOutput, calls=%fused_computation.6 | convolution fusion | flops 4294967296 | bytes 14680064 | tf_op jit(solution)/shard_map/axcy,cyz->xaz/dot_general | solution.py:55
  185.7 19.7 %custom-call.18 = f32[2,128,128]{1,2,0:T(8,128)S(1)} custom-call(f32[2,128,128]{2,1,0:T(8,128)S(1)} %get-tuple-element.22), custom_call_target="InvertDiagBlocksLowerTriangular" | custom-call | tf_op jit(solution)/shard_map/jit(_cho_solve)/triangular_solve | solution.py:16
  206.6 44.7 %all-reduce.7.cloned.1.call-done = f32[256,4,512]{2,0,1:T(8,128)} async-done(((f32[256,4,512]{2,0,1:T(8,128)}), f32[256,4,512]{2,0,1:T(8,128)}) %all-reduce.7.cloned.1.call-update) | async-done | bytes 2097168 | tf_op jit(solution)/shard_map/psum | solution.py:54
  251.3 1.0 fusion.15
  252.3 0.9 convolution_bitcast_fusion.3
  253.2 0.9 convolution_bitcast_fusion.2
  254.1 1.1 fusion.10
  255.2 0.9 convolution_bitcast_fusion.1
  256.8 66.2 %all-reduce.11.cloned.1.call-done = (f32[256,256]{1,0:T(8,128)}, f32[256,256]{1,0:T(8,128)}, f32[256,256]{1,0:T(8,128)}) async-done(((f32[256,256]{1,0:T(8,128)}, f32[256,256]{1,0:T(8,128)}, f32[256,256]{1,0:T(8,128)}), (f32[256,256]{1,0:T(8,128)}, f32[256,256]{1,0:T(8,128)}, f32[256,256]{1,0:T(8,128)})) %all-reduce.11.cloned.1.call-update) | async-done | bytes 786448 | tf_op jit(solution)/shard_map/psum | solution.py:9
  323.8 1.6 fusion.71
  325.5 152.1 %all-reduce.9.cloned.1.call-done = (f32[256,256]{1,0:T(8,128)}, f32[256,256]{1,0:T(8,128)}, f32[256,256]{1,0:T(8,128)}) async-done(((f32[256,256]{1,0:T(8,128)}, f32[256,256]{1,0:T(8,128)}, f32[256,256]{1,0:T(8,128)}), (f32[256,256]{1,0:T(8,128)}, f32[256,256]{1,0:T(8,128)}, f32[256,256]{1,0:T(8,128)})) %all-reduce.9.cloned.1.call-update) | async-done | bytes 786448 | tf_op jit(solution)/shard_map/psum | solution.py:9
  477.6 1.0 maximum_subtract_fusion
  478.6 1.2 fusion.7
  479.8 1.9 fusion.6
  (64 shorter events, 7.3 us)
Async XLA Ops:
  7.2 247.0 %copy-start = (bf16[256,256]{1,0:T(8,128)(2,1)S(1)}, bf16[256,256]{1,0:T(8,128)(2,1)}, u32[]{:S(2)}) copy-start(bf16[256,256]{1,0:T(8,128)(2,1)} %param.16) | copy-start | bytes 393220
  7.2 89.3 %all-gather.3.cloned.1.call-start = ((), (), s32[]{:S(2)}) async-start(), calls=%async_computation.2 | async-start | bytes 4325376 | tf_op jit(solution)/shard_map/all_gather | solution.py:49
  101.2 71.8 %all-to-all-start = ((bf16[4,4,8,32,512]{4,3,1,0,2:T(8,128)(2,1)}), bf16[4,4,8,32,512]{4,3,1,0,2:T(8,128)(2,1)}, u32[]{:S(2)}, u32[]{:S(2)}) async-start(bf16[4,4,8,32,512]{4,3,1,0,2:T(8,128)(2,1)} %copy.82), calls=%async_computation | async-start | bytes 8388608 | tf_op jit(solution)/shard_map/all_to_all | solution.py:51
  106.2 145.1 %all-reduce.7.cloned.1.call-start = ((), (), s32[]{:S(2)}) async-start(), calls=%async_computation.1 | async-start | bytes 4194304 | tf_op jit(solution)/shard_map/psum | solution.py:54
  185.4 137.6 %all-reduce.11.cloned.1.call-start = ((), (), s32[]{:S(2)}) async-start(), calls=%async_computation.4 | async-start | bytes 1572864 | tf_op jit(solution)/shard_map/psum | solution.py:9
  255.2 226.6 %copy-start.3 = (bf16[32,4,256]{2,0,1:T(8,128)(2,1)}, bf16[32,4,256]{2,0,1:T(8,128)(2,1)S(1)}, u32[]{:S(2)}) copy-start(bf16[32,4,256]{2,0,1:T(8,128)(2,1)S(1)} %fusion.10) | copy-start | bytes 196612
  256.2 221.4 %all-reduce.9.cloned.1.call-start = ((), (), s32[]{:S(2)}) async-start(), calls=%async_computation.3 | async-start | bytes 1572864 | tf_op jit(solution)/shard_map/psum | solution.py:9
  478.6 3.2 copy-start.1
  479.8 2.0 copy-start.2
Sparse Core Ops, SparseCore 0:
  11.6 84.8 all-gather.2
  185.5 65.7 all-reduce.6
  256.3 66.6 all-reduce.10
  327.0 150.5 all-reduce.8
